TPU v7x, 32 devices: a whole 2x2x4 slice. The times are simulated.
32 devices in a mesh: wide: 16 (over z, y, core), narrow: 2 (over x).
Axes of the slice: x: 2, y: 2, z: 4, core: 2. Of those that a mesh axis runs over, the one named last changes fastest.
Arguments:
- enc_hidden: bfloat16 [3072, 6144], P('wide', 'narrow'), may hold values from -6 to 6
- enc_gain: float32 [6144], P('narrow'), may hold values from 0.1 to 1.9
- cross_weight: bfloat16 [6144, 256], P('narrow'), may hold values from -0.078125 to 0.078125
- assign: int32 [16], P('wide'), may hold values from 0 to 1
- token_ids: int32 [16, 2, 64], P('wide'), may hold values from 0 to 7999, as said below
- cross_table: bfloat16 [8000, 6144], P('wide', 'narrow'), may hold values from -540 to 540
- self_table: bfloat16 [8000, 6144], P('wide', 'narrow'), may hold values from -540 to 540
- kv_table: bfloat16 [8000, 256], P('wide'), may hold values from -6 to 6
- self_cache: bfloat16 [16, 64, 768, 256], P('wide', 'narrow'), may hold values from -6 to 6
Outputs:
- cross_out: bfloat16 [16, 2, 64, 6144], P('wide', None, None, 'narrow')
- self_out: bfloat16 [16, 2, 64, 6144], P('wide', None, 'narrow')
Inputs may be any that keep to these rules, and one draw needn't show every extreme that they name: `token_ids`: within one group, at most 16 of its 128 ids lie in any one of the 16 ranges of 500 consecutive ids, and some range holds exactly 16 of them.
All inputs are finite; a program needn't handle non-finite values.
Results may differ from a plain program's by a relative error of at most 0.009.
The roundings to bfloat16 on the way count: a program that leaves them out, or rounds other values in their place, can miss the bound.
Values may be sent and summed in bfloat16 or wider, within the bound.
A program may use at most 128 MiB of HBM per device.

v0:
```python
import jax
import jax.numpy as jnp
from jax import lax
from jax.sharding import PartitionSpec as P

D = 6144
HEADS = 48
HEAD = 128
ENC_LEN = 1536


EPS = 1e-06


def body(
    enc_hidden,
    enc_gain,
    cross_weight,
    assign,
    token_ids,
    cross_table,
    self_table,
    kv_table,
    self_cache,
):
    hidden = enc_hidden.astype(jnp.float32)
    part_squares = jnp.sum(hidden * hidden, axis=1)
    scaled = (hidden * enc_gain).astype(jnp.bfloat16)
    part_proj = jnp.dot(scaled, cross_weight, preferred_element_type=jnp.float32)
    problem = assign[0]
    narrow_count = lax.axis_size("narrow")
    narrow_index = lax.axis_index("narrow")
    heads_dev = HEADS // narrow_count
    factor = HEAD ** (-0.5)
    projected, squares = lax.psum((part_proj, part_squares), "narrow")
    enc_kv = (projected * lax.rsqrt(squares / D + EPS)[:, None]).astype(jnp.bfloat16)
    gathered = lax.all_gather(enc_kv, "wide", axis=0, tiled=True)
    span = ENC_LEN
    problem_kv = lax.dynamic_slice_in_dim(gathered, problem * span, span, 0)
    keys = problem_kv[:, :HEAD]
    values = problem_kv[:, HEAD:]
    wide_count = lax.axis_size("wide")
    per_owner = cross_table.shape[0]
    steps = token_ids.shape[1]
    cand = token_ids.shape[2]
    capacity = max(2, 2 * steps * cand // wide_count)
    flat = token_ids.reshape(-1)
    owner = flat // per_owner
    local = flat - owner * per_owner
    owner_hits = (owner[:, None] == jnp.arange(wide_count, dtype=jnp.int32)[None, :]).astype(
        jnp.int32
    )
    earlier = jnp.cumsum(owner_hits, axis=0) - owner_hits
    rank = jnp.sum(earlier * owner_hits, axis=1)
    target = owner * capacity + rank
    slot_match = target[None, :] == jnp.arange(wide_count * capacity, dtype=jnp.int32)[:, None]
    filled = jnp.any(slot_match, axis=1)
    request = jnp.where(filled, jnp.sum(jnp.where(slot_match, local[None, :], 0), axis=1), -1)
    asked = lax.all_to_all(
        request.reshape(wide_count, capacity), "wide", split_axis=0, concat_axis=0, tiled=True
    ).reshape(-1)
    valid = asked >= 0
    index = jnp.where(valid, asked, 0)

    def lookup(table):
        rows = jnp.take(table, index, axis=0)
        rows = jnp.where(valid[:, None], rows, jnp.zeros((), table.dtype))
        return rows.reshape(wide_count, capacity, table.shape[1])

    returned = (
        lax.all_to_all(lookup(cross_table), "wide", split_axis=0, concat_axis=0, tiled=True),
        lax.all_to_all(lookup(self_table), "wide", split_axis=0, concat_axis=0, tiled=True),
        lax.all_to_all(lookup(kv_table), "wide", split_axis=0, concat_axis=0, tiled=True),
    )
    cross_q, self_q, new_kv = [
        jnp.take(piece.reshape(wide_count * capacity, piece.shape[2]), target, axis=0)
        for piece in returned
    ]
    rows_total = steps * cand
    own_q = cross_q.reshape(rows_total, heads_dev, HEAD)
    scores = jnp.einsum("rhd,kd->rhk", own_q, keys, preferred_element_type=jnp.float32) * factor
    peak = jnp.max(scores, axis=-1, keepdims=True)
    expo = jnp.exp(scores - peak)
    total = jnp.sum(expo, axis=-1)
    result = (
        jnp.einsum(
            "rhk,kd->rhd", expo.astype(jnp.bfloat16), values, preferred_element_type=jnp.float32
        )
        / total[..., None]
    )
    cross_out = result.astype(jnp.bfloat16).reshape(1, steps, cand, heads_dev * HEAD)
    own_cand = cand // narrow_count
    queries = lax.all_to_all(
        self_q.reshape(steps, cand, self_q.shape[1]),
        "narrow",
        split_axis=1,
        concat_axis=2,
        tiled=True,
    )
    queries = queries.reshape(steps, own_cand, HEADS, HEAD)
    fresh = lax.dynamic_slice_in_dim(
        new_kv.reshape(steps, cand, new_kv.shape[1]), narrow_index * own_cand, own_cand, 1
    )
    cache = self_cache[0]
    prefix_scores = (
        jnp.einsum("tchd,cpd->tchp", queries, cache[..., :HEAD], preferred_element_type=jnp.float32)
        * factor
    )
    fresh_scores = (
        jnp.einsum("tchd,jcd->tchj", queries, fresh[..., :HEAD], preferred_element_type=jnp.float32)
        * factor
    )
    step_index = jnp.arange(steps, dtype=jnp.int32)
    allowed = (step_index[None, :] <= step_index[:, None])[:, None, None, :]
    fresh_masked = jnp.where(allowed, fresh_scores, -jnp.inf)
    peak = jnp.maximum(jnp.max(prefix_scores, axis=-1), jnp.max(fresh_masked, axis=-1))[..., None]
    prefix_expo = jnp.exp(prefix_scores - peak)
    fresh_expo = jnp.where(allowed, jnp.exp(fresh_masked - peak), 0.0)
    total = jnp.sum(prefix_expo, axis=-1) + jnp.sum(fresh_expo, axis=-1)
    summed = jnp.einsum(
        "tchp,cpd->tchd",
        prefix_expo.astype(jnp.bfloat16),
        cache[..., HEAD:],
        preferred_element_type=jnp.float32,
    )
    summed = summed + jnp.einsum(
        "tchj,jcd->tchd",
        fresh_expo.astype(jnp.bfloat16),
        fresh[..., HEAD:],
        preferred_element_type=jnp.float32,
    )
    self_result = summed / total[..., None]
    self_out = self_result.astype(jnp.bfloat16).reshape(1, steps, own_cand, HEADS * HEAD)
    return (cross_out, self_out)


def solution(mesh):
    placed = (
        P("wide", "narrow"),
        P("narrow"),
        P("narrow", None),
        P("wide"),
        P("wide", None, None),
        P("wide", "narrow"),
        P("wide", "narrow"),
        P("wide", None),
        P("wide", "narrow", None, None),
    )
    return jax.shard_map(
        body,
        mesh=mesh,
        in_specs=placed,
        out_specs=(P("wide", None, None, "narrow"), P("wide", None, "narrow", None)),
        check_vma=False,
    )
```

profile of v0, /device:TPU:0, one launch (start us, length us, event | category | flops | bytes accessed | tf_op | source)
XLA Modules:
  0.0 216.8 jit_solution(11326258316219212226)
XLA Ops:
  7.2 0.9 reshape.298
  8.9 13.7 %all_to_all.36 = s32[16,1,16]{2,1,0:T(1,128)S(1)} all-to-all(s32[16,1,16]{2,1,0:T(1,128)S(1)} %select_n.148), channel_id=1, replica_groups=mesh['wide'=16,'narrow'=2] {'wide'}, dimensions={0} | all-to-all | bytes 2048 | tf_op jit(solution)/shard_map/all_to_all | solution.py:59
  24.0 2.0 gather_fusion
  25.9 0.8 select_select_fusion.2
  26.7 3.5 %all-to-all-start.4 = ((bf16[16,16,256]{2,1,0:T(8,128)(2,1)}), bf16[16,16,256]{2,1,0:T(8,128)(2,1)S(1)}, u32[]{:S(2)}, u32[]{:S(2)}) async-start(bf16[16,16,256]{2,1,0:T(8,128)(2,1)} %select_select_fusion.2), calls=%async_computation.4 | async-start | bytes 262144 | tf_op jit(solution)/shard_map/all_to_all | solution.py:73
  30.2 2.7 %gather_fusion.4 = bf16[256,3072]{1,0:T(8,128)(2,1)} fusion(bf16[500,3072]{1,0:T(8,128)(2,1)S(1)} %copy-done, s32[1024]{0:T(1024)S(1)} %pad_clamp_fusion.3), kind=kCustom, calls=%fused_computation.2.clone | custom fusion | bytes 3146752 | tf_op jit(solution)/shard_map/jit(_take)/gather | solution.py:66
  33.0 6.7 %gather_fusion.2 = bf16[256,3072]{1,0:T(8,128)(2,1)} fusion(bf16[500,3072]{1,0:T(8,128)(2,1)} %param.18, s32[1024]{0:T(1024)S(1)} %pad_clamp_fusion.3), kind=kCustom, calls=%fused_computation.clone | custom fusion | bytes 3146752 | tf_op jit(solution)/shard_map/jit(_take)/gather | solution.py:66
  39.7 3.5 %select_select_fusion = (bf16[256,3072]{1,0:T(8,128)(2,1)}, bf16[256,3072]{1,0:T(8,128)(2,1)}) fusion(bf16[256,3072]{1,0:T(8,128)(2,1)S(1)} %copy-done.2, pred[256]{0:T(512)(128)(4,1)S(1)} %get-tuple-element.17, pred[256]{0:T(512)(128)(4,1)S(1)} %get-tuple-element.25, bf16[256,3072]{1,0:T(8,128)(2,1)} %gather_fusion.2), kind=kLoop, calls=%fused_computation.29 | loop fusion | flops 3145728 | bytes 6291968 | tf_op jit(solution)/shard_map/jit(_where)/select_n | solution.py:67
  43.1 42.0 %all_to_all.37 = bf16[16,16,3072]{2,1,0:T(8,128)(2,1)} all-to-all(bf16[16,16,3072]{2,1,0:T(8,128)(2,1)} %bitcast.113), channel_id=1, replica_groups=mesh['wide'=16,'narrow'=2] {'wide'}, dimensions={0} | all-to-all | bytes 3145728 | tf_op jit(solution)/shard_map/all_to_all | solution.py:71
  85.1 5.2 %all-to-all-start.2 = ((bf16[16,16,3072]{2,1,0:T(8,128)(2,1)}), bf16[16,16,3072]{2,1,0:T(8,128)(2,1)S(1)}, u32[]{:S(2)}, u32[]{:S(2)}) async-start(bf16[16,16,3072]{2,1,0:T(8,128)(2,1)} %bitcast.112), calls=%async_computation.2 | async-start | bytes 3145728 | tf_op jit(solution)/shard_map/all_to_all | solution.py:72
  90.4 2.6 %fusion.18 = f32[192,256]{1,0:T(8,128)} fusion(bf16[3072,256]{1,0:T(8,128)(2,1)} %param.15, bf16[192,3072]{1,0:T(8,128)(2,1)S(1)} %copy-done.3, f32[3072]{0:T(1024)S(1)} %copy-done.5), kind=kOutput, calls=%fused_computation.32 | convolution fusion | flops 303759360 | bytes 2961408 | tf_op jit(solution)/shard_map/dot_general | solution.py:29
  93.4 4.9 %psum.15 = f32[192]{0:T(256)S(1)} all-reduce(f32[192]{0:T(256)S(1)} %fusion.13), channel_id=1, replica_groups=mesh['wide'=16,'narrow'=2] {'narrow'}, use_global_device_ids=true, to_apply=%region_6.9 | all-reduce | flops 192 | bytes 1536 | tf_op jit(solution)/shard_map/psum | solution.py:35
  98.3 19.5 %all-reduce.2.cloned.1.call-done = f32[192,256]{1,0:T(8,128)} async-done(((f32[192,256]{1,0:T(8,128)}), f32[192,256]{1,0:T(8,128)}) %all-reduce.2.cloned.1.call-update) | async-done | bytes 196624 | tf_op jit(solution)/shard_map/psum | solution.py:35
  117.8 1.7 multiply_convert_fusion
  120.6 0.8 gather_fusion.1
  121.6 3.4 %gather_fusion.3 = bf16[128,3072]{1,0:T(8,128)(2,1)S(1)} fusion(bf16[256,3072]{1,0:T(8,128)(2,1)} %bitcast.111, s32[1024]{0:T(1024)S(1)} %pad_clamp_fusion.2), kind=kCustom, calls=%fused_computation.1.clone | custom fusion | bytes 1573376 | tf_op jit(solution)/shard_map/jit(_take)/gather | solution.py:76
  125.1 1.9 gather_fusion.5
  127.0 1.3 broadcast_select_fusion
  128.3 1.7 copy.30
  130.0 3.7 %all-to-all-start.3 = ((bf16[2,64,3072]{2,0,1:T(2,128)(2,1)}), bf16[2,64,3072]{2,0,1:T(2,128)(2,1)S(1)}, u32[]{:S(2)}, u32[]{:S(2)}) async-start(bf16[2,64,3072]{2,0,1:T(2,128)(2,1)} %copy.30), calls=%async_computation.3 | async-start | bytes 1572864 | tf_op jit(solution)/shard_map/all_to_all | solution.py:93
  133.7 26.5 %all-gather.2.cloned.1.call-done = bf16[3072,256]{1,0:T(8,128)(2,1)} async-done(((bf16[192,256]{1,0:T(8,128)(2,1)}), bf16[3072,256]{1,0:T(8,128)(2,1)}) %all-gather.2.cloned.1.call-update) | async-done | bytes 1572880 | tf_op jit(solution)/shard_map/all_gather | solution.py:37
  160.3 8.9 %multiply_reduce_fusion = (f32[128,24]{0,1:T(8,128)S(1)}, f32[128,24,1536]{2,0,1:T(8,128)}) fusion(bf16[3072,256]{1,0:T(8,128)(2,1)} %all-gather.2.cloned.1.call-done, s32[]{:T(128)S(6)} %select_n.151, bf16[16,24,8,128]{3,2,1,0:T(8,128)(2,1)S(1)} %get-tuple-element.27), kind=kOutput, calls=%fused_computation.7 | convolution fusion | flops 1217393664 | bytes 20066308 | tf_op jit(solution)/shard_map/rhd,kd->rhk/dot_general | solution.py:81
  169.1 9.6 %fusion = f32[128,24]{0,1:T(8,128)S(1)} fusion(f32[128,24,1536]{2,0,1:T(8,128)} %get-tuple-element.29, f32[128,24]{0,1:T(8,128)S(1)} %get-tuple-element.28), kind=kLoop, calls=%fused_computation.8 | loop fusion | flops 14152704 | bytes 18898944 | tf_op jit(solution)/shard_map/reduce_sum | solution.py:84
  178.7 8.3 %divide_convert_fusion = bf16[128,24,128]{2,0,1:T(8,128)(2,1)S(1)} fusion(f32[128,24,1536]{2,0,1:T(8,128)} %get-tuple-element.29, f32[128,24]{0,1:T(8,128)S(1)} %get-tuple-element.28, f32[128,24]{0,1:T(8,128)S(1)} %fusion, bf16[3072,256]{1,0:T(8,128)(2,1)} %all-gather.2.cloned.1.call-done, s32[]{:T(128)S(6)} %select_n.151, s32[]{:T(128)S(6)} %add.157), kind=kOutput, calls=%fused_computation.31 | convolution fusion | flops 1222901760 | bytes 20078600 | tf_op jit(solution)/shard_map/rhk,kd->rhd/dot_general | solution.py:86
  187.6 1.2 reshape.303
  188.9 0.8 copy.32
  190.3 5.0 %bitcast_reduce_fusion = (f32[2,32,48]{2,0,1:T(2,128)S(1)}, f32[32,2,48,768]{3,2,1,0:T(8,128)S(1)}) fusion(bf16[2,32,48,128]{3,2,0,1:T(8,128)(2,1)S(1)} %reshape.307, bf16[32,768,256]{2,1,0:T(8,128)(2,1)} %bitcast.116), kind=kOutput, calls=%fused_computation.11 | convolution fusion | flops 608695296 | bytes 16527360 | tf_op jit(solution)/shard_map/tchd,cpd->tchp/dot_general | solution.py:106
  195.3 0.9 fusion.42
  196.9 2.3 %fusion.5 = f32[2,32,48]{2,0,1:T(2,128)S(1)} fusion(f32[32,2,48,768]{3,2,1,0:T(8,128)S(1)} %get-tuple-element.31, f32[2,32,48]{2,0,1:T(2,128)S(1)} %max.7), kind=kLoop, calls=%fused_computation.14 | loop fusion | flops 7074816 | bytes 9461760 | tf_op jit(solution)/shard_map/reduce_sum | solution.py:119
  199.2 5.7 %fusion.15 = bf16[2,32,48,128]{3,2,0,1:T(8,128)(2,1)} fusion(f32[32,128,2,48]{1,3,2,0:T(8,128)S(1)} %fusion.30, bf16[32,768,256]{2,1,0:T(8,128)(2,1)} %bitcast.117, f32[32,2,48,768]{3,2,1,0:T(8,128)S(1)} %get-tuple-element.31, f32[2,32,48]{2,0,1:T(2,128)S(1)} %max.7, f32[2,32,48]{2,0,1:T(2,128)S(1)} %add.140), kind=kOutput, calls=%fused_computation.28 | convolution fusion | flops 612237312 | bytes 18112512 | tf_op jit(solution)/shard_map/tchp,cpd->tchd/dot_general | solution.py:120
  204.9 2.8 %reshape.311 = bf16[1,2,32,6144]{3,1,2,0:T(2,128)(2,1)} reshape(bf16[2,32,48,128]{3,2,0,1:T(8,128)(2,1)} %fusion.15) | data formatting | bytes 1572864 | tf_op jit(solution)/shard_map/reshape | solution.py:133
  207.7 2.2 %copy.35 = bf16[1,2,32,6144]{3,2,1,0:T(8,128)(2,1)} copy(bf16[1,2,32,6144]{3,1,2,0:T(2,128)(2,1)} %reshape.311) | data formatting | bytes 1572864
  (59 shorter events, 5.1 us)
Async XLA Ops:
  7.2 23.1 %copy-start = (bf16[500,3072]{1,0:T(8,128)(2,1)S(1)}, bf16[500,3072]{1,0:T(8,128)(2,1)}, u32[]{:S(2)}) copy-start(bf16[500,3072]{1,0:T(8,128)(2,1)} %param.19) | copy-start | bytes 9216004
  26.7 16.4 %all-to-all-start.4 = ((bf16[16,16,256]{2,1,0:T(8,128)(2,1)}), bf16[16,16,256]{2,1,0:T(8,128)(2,1)S(1)}, u32[]{:S(2)}, u32[]{:S(2)}) async-start(bf16[16,16,256]{2,1,0:T(8,128)(2,1)} %select_select_fusion.2), calls=%async_computation.4 | async-start | bytes 262144 | tf_op jit(solution)/shard_map/all_to_all | solution.py:73
  33.0 6.7 %copy-start.2 = (bf16[256,3072]{1,0:T(8,128)(2,1)S(1)}, bf16[256,3072]{1,0:T(8,128)(2,1)}, u32[]{:S(2)}) copy-start(bf16[256,3072]{1,0:T(8,128)(2,1)} %gather_fusion.4) | copy-start | bytes 4718596
  85.1 5.3 %copy-start.3 = (bf16[192,3072]{1,0:T(8,128)(2,1)S(1)}, bf16[192,3072]{1,0:T(8,128)(2,1)}, u32[]{:S(2)}) copy-start(bf16[192,3072]{1,0:T(8,128)(2,1)} %param.13) | copy-start | bytes 3538948
  85.1 5.3 %copy-start.5 = (f32[3072]{0:T(1024)S(1)}, f32[3072]{0:T(1024)}, u32[]{:S(2)}) copy-start(f32[3072]{0:T(1024)} %param.14) | copy-start | bytes 36868
  85.1 39.9 %all-to-all-start.2 = ((bf16[16,16,3072]{2,1,0:T(8,128)(2,1)}), bf16[16,16,3072]{2,1,0:T(8,128)(2,1)S(1)}, u32[]{:S(2)}, u32[]{:S(2)}) async-start(bf16[16,16,3072]{2,1,0:T(8,128)(2,1)} %bitcast.112), calls=%async_computation.2 | async-start | bytes 3145728 | tf_op jit(solution)/shard_map/all_to_all | solution.py:72
  90.3 29.9 %copy-start.4 = (s32[1,2,64]{2,1,0:T(2,128)S(1)}, s32[1,2,64]{2,1,0:T(2,128)}, u32[]{:S(2)}) copy-start(s32[1,2,64]{2,1,0:T(2,128)} %param.17) | copy-start | bytes 1540
  90.4 27.4 %all-reduce.2.cloned.1.call-start = ((), (), s32[]{:S(2)}) async-start(), calls=%async_computation.5 | async-start | bytes 393216 | tf_op jit(solution)/shard_map/psum | solution.py:35
  93.0 67.3 %all-gather.2.cloned.1.call-start = ((), (), s32[]{:S(2)}) async-start(), calls=%async_computation.6 | async-start | bytes 1671168 | tf_op jit(solution)/shard_map/all_gather | solution.py:37
  130.0 58.8 %all-to-all-start.3 = ((bf16[2,64,3072]{2,0,1:T(2,128)(2,1)}), bf16[2,64,3072]{2,0,1:T(2,128)(2,1)S(1)}, u32[]{:S(2)}, u32[]{:S(2)}) async-start(bf16[2,64,3072]{2,0,1:T(2,128)(2,1)} %copy.30), calls=%async_computation.3 | async-start | bytes 1572864 | tf_op jit(solution)/shard_map/all_to_all | solution.py:93
  199.2 10.7 %copy-start.1 = (bf16[500,3072]{1,0:T(8,128)(2,1)S(1)}, bf16[500,3072]{1,0:T(8,128)(2,1)}, u32[]{:S(2)}) copy-start(bf16[500,3072]{1,0:T(8,128)(2,1)} %param.19) | copy-start | bytes 9216004
Sparse Core Ops, SparseCore 0:
  94.0 23.7 all-reduce.1
  120.6 39.5 all-gather.1
where the time goes:
time: 218 us; the launch traced here: 217 us
  blocking collectives  60.6 us (28%)
  waiting for transfers between devices  46 us (21%)
  matrix products  31.8 us (15%)
  local copies, waits for them, and re-layouts  29.5 us (14%)
  other arithmetic  21.3 us (10%)
  between operations  15 us (7%)
  starting transfers between devices  12.5 us (6%)
    all_to_all x1, blocking collectives, body(): lax.all_to_all(lookup(cross_table), 'wide', split_axis=0, concat_axis=0,...  42 us
    all_gather x1, waiting for transfers between devices, body(): gathered = lax.all_gather(enc_kv, 'wide', axis=0, tiled=True)  26.5 us
    psum x1, waiting for transfers between devices, body(): projected, squares = lax.psum((part_proj, part_squares), 'narrow')  19.5 us
    all_to_all x1, blocking collectives, body(): lax.all_to_all(request.reshape(wide_count, capacity), 'wide', split_axis=...  13.7 us
    gather x3, local copies, waits for them, and re-layouts, lookup(): rows = jnp.take(table, index, axis=0)  11.3 us
    reduce_sum x1, other arithmetic, body(): total = jnp.sum(expo, axis=-1)  9.6 us
    dot_general x1, matrix products, body(): jnp.einsum('rhd,kd->rhk', own_q, keys, preferred_element_type=jnp.float32)  8.86 us
    dot_general x1, matrix products, body(): jnp.einsum('rhk,kd->rhd', expo.astype(jnp.bfloat16), values, preferred_el...  8.3 us
  transfers between devices with their start and end apart: 5, of which 2 were waited for; matrix products, arithmetic and copies ran while one was open for 26% of the time, Pallas kernels for 0%

commit v1 on v0

v1 whole, which is shorter than its diff:
```python
import functools
import math

import jax
import jax.numpy as jnp
from jax import lax
from jax.experimental import pallas as pl
from jax.experimental.pallas import tpu as pltpu
from jax.sharding import PartitionSpec as P

D = 6144
HEADS = 48
HEAD = 128
ENC_LEN = 1536
EPS = 1e-06
TILE_ROWS = 16
SCALE = HEAD ** (-0.5) * math.log2(math.e)

MESH_ID = pl.DeviceIdType.MESH
DOT_T = (((1,), (1,)), ((), ()))


def greet(wide, narrow):
    me = lax.axis_index("wide")
    side = lax.axis_index("narrow")
    barrier = pltpu.get_barrier_semaphore()

    @pl.loop(1, wide)
    def _(step):
        pl.semaphore_signal(
            barrier, inc=1, device_id={"wide": lax.rem(me + step, wide)}, device_id_type=MESH_ID
        )

    for step in range(1, narrow):
        pl.semaphore_signal(
            barrier,
            inc=1,
            device_id={"narrow": lax.rem(side + step, narrow)},
            device_id_type=MESH_ID,
        )
    pl.semaphore_wait(barrier, wide + narrow - 2)


def exchange_kernel(
    wide, narrow, ids_ref, part_ref, ids_out, parts_out, id_send, id_recv, part_send, part_recv
):
    me = lax.axis_index("wide")
    side = lax.axis_index("narrow")
    greet(wide, narrow)

    def ids_copy(step):
        return pltpu.make_async_remote_copy(
            src_ref=ids_ref,
            dst_ref=ids_out.at[me],
            send_sem=id_send.at[step],
            recv_sem=id_recv.at[step],
            device_id={"wide": lax.rem(me + step, wide)},
            device_id_type=MESH_ID,
        )

    def part_copy(step):
        return pltpu.make_async_remote_copy(
            src_ref=part_ref,
            dst_ref=parts_out.at[step - 1],
            send_sem=part_send.at[step],
            recv_sem=part_recv.at[step],
            device_id={"narrow": lax.rem(side + step, narrow)},
            device_id_type=MESH_ID,
        )

    @pl.loop(1, wide)
    def _(step):
        ids_copy(step).start()

    for step in range(1, narrow):
        part_copy(step).start()
    ids_out[me] = ids_ref[...]

    @pl.loop(1, wide)
    def _(step):
        ids_copy(step).wait()

    for step in range(1, narrow):
        part_copy(step).wait()


def exchange(ids, part, wide, narrow):
    vmem = pl.BlockSpec(memory_space=pltpu.VMEM)
    return pl.pallas_call(
        functools.partial(exchange_kernel, wide, narrow),
        out_shape=(
            jax.ShapeDtypeStruct((wide,) + ids.shape, ids.dtype),
            jax.ShapeDtypeStruct((narrow - 1,) + part.shape, part.dtype),
        ),
        in_specs=[vmem, vmem],
        out_specs=(vmem, vmem),
        scratch_shapes=[
            pltpu.SemaphoreType.DMA((wide,)),
            pltpu.SemaphoreType.DMA((wide,)),
            pltpu.SemaphoreType.DMA((narrow,)),
            pltpu.SemaphoreType.DMA((narrow,)),
        ],
        compiler_params=pltpu.CompilerParams(collective_id=0, has_side_effects=True),
    )(ids, part)


def main_kernel(
    dims,
    problem_ref,
    enc_ref,
    cross_ref,
    self_ref,
    kv_ref,
    cache_ref,
    perm_cross_ref,
    perm_self_ref,
    cross_out,
    self_out,
    enc_buf,
    keys,
    cross_raw,
    self_raw,
    kv_raw,
    cache,
    fresh,
    q_rows,
    o_rows,
    local_sem,
    enc_send,
    enc_recv,
    self_send,
    self_recv,
    kv_send,
    kv_recv,
    cross_send,
    cross_recv,
    side_send,
    side_recv,
):
    wide, narrow, steps, own, problems, chunks = dims
    me = lax.axis_index("wide")
    side = lax.axis_index("narrow")
    levels = wide.bit_length() - 1
    enc_rows = enc_ref.shape[0]
    features = cross_ref.shape[1]
    heads_dev = features // HEAD
    chunk_cols = features // chunks
    cap = cross_ref.shape[0] // wide

    place = 0
    for bit in range(levels):
        place = place + ((me // 2**bit) % 2) * 2 ** (levels - 1 - bit)

    def rows_of(device):
        return pl.ds(pl.multiple_of(device * cap, cap), cap)

    def enc_copy(level):
        reach = 2 ** (levels - 1 - level)
        bit = (me // reach) % 2
        start = (place // 2**level) * 2**level
        block = pl.ds(pl.multiple_of(start * enc_rows, enc_rows), 2**level * enc_rows)
        return pltpu.make_async_remote_copy(
            src_ref=enc_buf.at[block],
            dst_ref=enc_buf.at[block],
            send_sem=enc_send.at[level],
            recv_sem=enc_recv.at[level],
            device_id={"wide": me + reach * (1 - 2 * bit)},
            device_id_type=MESH_ID,
        )

    def row_copy(src, dst, send, recv, step):
        peer = lax.rem(me + step, wide)
        return pltpu.make_async_remote_copy(
            src_ref=src.at[rows_of(peer)],
            dst_ref=dst.at[rows_of(me)],
            send_sem=send.at[step],
            recv_sem=recv.at[step],
            device_id={"wide": peer},
            device_id_type=MESH_ID,
        )

    def self_copy(step):
        return row_copy(self_ref, self_raw.at[side], self_send, self_recv, step)

    def kv_copy(step):
        return row_copy(kv_ref, kv_raw, kv_send, kv_recv, step)

    def cross_copy(step, chunk):
        peer = lax.rem(me + step, wide)
        cols = pl.ds(chunk * chunk_cols, chunk_cols)
        return pltpu.make_async_remote_copy(
            src_ref=cross_ref.at[rows_of(peer), cols],
            dst_ref=cross_raw.at[rows_of(me), cols],
            send_sem=cross_send.at[chunk, step],
            recv_sem=cross_recv.at[chunk, step],
            device_id={"wide": peer},
            device_id_type=MESH_ID,
        )

    def side_copy(step, hop):
        rows = rows_of(lax.rem(me - step + wide, wide))
        return pltpu.make_async_remote_copy(
            src_ref=self_raw.at[side, rows],
            dst_ref=self_raw.at[side, rows],
            send_sem=side_send.at[hop - 1, step],
            recv_sem=side_recv.at[hop - 1, step],
            device_id={"narrow": lax.rem(side + hop, narrow)},
            device_id_type=MESH_ID,
        )

    own_block = rows_of(me)
    locals_ = [
        pltpu.make_async_copy(
            enc_ref,
            enc_buf.at[pl.ds(pl.multiple_of(place * enc_rows, enc_rows), enc_rows)],
            local_sem.at[0],
        ),
        pltpu.make_async_copy(
            self_ref.at[own_block], self_raw.at[side, own_block], local_sem.at[1]
        ),
        pltpu.make_async_copy(kv_ref.at[own_block], kv_raw.at[own_block], local_sem.at[2]),
        pltpu.make_async_copy(cross_ref.at[own_block], cross_raw.at[own_block], local_sem.at[3]),
        pltpu.make_async_copy(cache_ref, cache, local_sem.at[4]),
    ]
    for copy in locals_:
        copy.start()
    greet(wide, narrow)
    locals_[0].wait()
    enc_copy(0).start()

    @pl.loop(1, wide)
    def _(step):
        kv_copy(step).start()

    bounds = [1 + (wide - 1) * level // levels for level in range(levels + 1)]
    for level in range(levels):

        @pl.loop(bounds[level], bounds[level + 1])
        def _(step):
            self_copy(step).start()

        enc_copy(level).wait()
        if level + 1 < levels:
            enc_copy(level + 1).start()

    locals_[1].wait()
    for hop in range(1, narrow):
        side_copy(0, hop).start()

    @pl.loop(1, wide)
    def _(step):
        self_copy(step).wait_recv()
        for hop in range(1, narrow):
            side_copy(step, hop).start()
        for chunk in range(chunks):
            cross_copy(step, chunk).start()

    problem = problem_ref[0]
    problem_bits = problems.bit_length() - 1
    for block in range(wide // problems):
        mine = None
        for other in range(problems):
            turned = sum((other >> bit) % 2 << (problem_bits - 1 - bit) for bit in range(problem_bits))
            start = (block * problems + turned) * enc_rows
            rows = enc_buf[start : start + enc_rows, :]
            mine = rows if mine is None else jnp.where(problem == other, rows, mine)
        keys[block * enc_rows : (block + 1) * enc_rows, :] = mine

    locals_[2].wait()

    @pl.loop(1, wide)
    def _(step):
        kv_copy(step).wait()

    fresh[...] = jnp.dot(perm_self_ref[...], kv_raw[...], preferred_element_type=jnp.float32)

    @pl.loop(0, wide)
    def _(step):
        for hop in range(1, narrow):
            side_copy(step, hop).wait()

    total_rows = steps * own
    for part in range(narrow):

        @pl.loop(0, heads_dev)
        def _(head):
            cols = pl.ds(pl.multiple_of(head * HEAD, HEAD), HEAD)
            moved = jnp.dot(
                perm_self_ref[...], self_raw[part, :, cols], preferred_element_type=jnp.float32
            )
            start = pl.multiple_of((part * heads_dev + head) * total_rows, total_rows)
            q_rows[pl.ds(start, total_rows), :] = moved

    locals_[4].wait()

    @pl.loop(0, own, unroll=2)
    def _(cand):
        rows = [
            q_rows[pl.ds(step * own + cand, HEADS, stride=total_rows), :] for step in range(steps)
        ]
        query = jnp.concatenate(rows, axis=0)
        scores = lax.dot_general(
            query.astype(jnp.bfloat16),
            cache[cand, :, :HEAD],
            DOT_T,
            preferred_element_type=jnp.float32,
        )
        row_step = lax.broadcasted_iota(jnp.int32, (steps * HEADS, 1), 0) // HEADS
        peak = jnp.max(scores, axis=1, keepdims=True)
        new = []
        for step in range(steps):
            row = fresh[pl.ds(step * own + cand, 1), :]
            score = jnp.sum(query * row[:, :HEAD], axis=1, keepdims=True)
            score = jnp.where(row_step >= step, score, -jnp.inf)
            peak = jnp.maximum(peak, score)
            new.append((row, score))
        expo = jnp.exp2((scores - peak) * SCALE)
        total = jnp.sum(expo, axis=1, keepdims=True)
        result = jnp.dot(
            expo.astype(jnp.bfloat16), cache[cand, :, HEAD:], preferred_element_type=jnp.float32
        )
        for row, score in new:
            weight = jnp.exp2((score - peak) * SCALE)
            total = total + weight
            result = result + weight.astype(jnp.bfloat16).astype(jnp.float32) * row[:, HEAD:]
        result = result / total
        for step in range(steps):
            o_rows[pl.ds(step * own + cand, HEADS, stride=total_rows), :] = result[
                step * HEADS : (step + 1) * HEADS
            ]

    @pl.loop(0, HEADS)
    def _(head):
        start = pl.multiple_of(head * total_rows, total_rows)
        cols = pl.ds(pl.multiple_of(head * HEAD, HEAD), HEAD)
        self_out[:, cols] = o_rows[pl.ds(start, total_rows), :].astype(jnp.bfloat16)

    locals_[3].wait()
    query_rows = perm_cross_ref.shape[0]
    group = math.gcd(heads_dev // chunks, 4)
    for chunk in range(chunks):

        @pl.loop(1, wide)
        def _(step):
            cross_copy(step, chunk).wait_recv()

        @pl.loop(0, heads_dev // chunks // group)
        def _(index):
            start = pl.multiple_of(chunk * chunk_cols + index * group * HEAD, HEAD)
            cols = pl.ds(start, group * HEAD)
            moved = jnp.dot(
                perm_cross_ref[...], cross_raw[:, cols], preferred_element_type=jnp.float32
            ).astype(jnp.bfloat16)
            query = jnp.concatenate(
                [moved[:, head * HEAD : (head + 1) * HEAD] for head in range(group)], axis=0
            )
            scores = lax.dot_general(
                query, keys[:, :HEAD], DOT_T, preferred_element_type=jnp.float32
            )
            peak = jnp.max(scores, axis=1, keepdims=True)
            expo = jnp.exp2((scores - peak) * SCALE)
            total = jnp.sum(expo, axis=1, keepdims=True)
            result = jnp.dot(
                expo.astype(jnp.bfloat16), keys[:, HEAD:], preferred_element_type=jnp.float32
            )
            result = (result / total).astype(jnp.bfloat16)
            cross_out[:, cols] = jnp.concatenate(
                [result[head * query_rows : (head + 1) * query_rows] for head in range(group)],
                axis=1,
            )

    @pl.loop(1, wide)
    def _(step):
        self_copy(step).wait_send()
        for chunk in range(chunks):
            cross_copy(step, chunk).wait_send()


def attend(problem, enc, cross_rows, self_rows, kv_rows, cache, perm_cross, perm_self, dims):
    wide, narrow, steps, own, problems, chunks = dims
    slots, features = cross_rows.shape
    enc_rows, kv_cols = enc.shape
    levels = wide.bit_length() - 1
    vmem = pl.BlockSpec(memory_space=pltpu.VMEM)
    anywhere = pl.BlockSpec(memory_space=pl.ANY)
    total_rows = steps * own
    bf16 = jnp.bfloat16
    dma = pltpu.SemaphoreType.DMA
    return pl.pallas_call(
        functools.partial(main_kernel, dims),
        out_shape=(
            jax.ShapeDtypeStruct((perm_cross.shape[0], features), bf16),
            jax.ShapeDtypeStruct((total_rows, HEADS * HEAD), bf16),
        ),
        in_specs=[
            pl.BlockSpec(memory_space=pltpu.SMEM),
            anywhere,
            anywhere,
            anywhere,
            anywhere,
            anywhere,
            vmem,
            vmem,
        ],
        out_specs=(vmem, vmem),
        scratch_shapes=[
            pltpu.VMEM((wide * enc_rows, kv_cols), bf16),
            pltpu.VMEM((wide // problems * enc_rows, kv_cols), bf16),
            pltpu.VMEM((slots, features), bf16),
            pltpu.VMEM((narrow, slots, features), bf16),
            pltpu.VMEM((slots, kv_cols), bf16),
            pltpu.VMEM(cache.shape, bf16),
            pltpu.VMEM((total_rows, kv_cols), jnp.float32),
            pltpu.VMEM((HEADS * total_rows, HEAD), jnp.float32),
            pltpu.VMEM((HEADS * total_rows, HEAD), jnp.float32),
            dma((5,)),
            dma((levels,)),
            dma((levels,)),
            dma((wide,)),
            dma((wide,)),
            dma((wide,)),
            dma((wide,)),
            dma((chunks, wide)),
            dma((chunks, wide)),
            dma((narrow - 1, wide)),
            dma((narrow - 1, wide)),
        ],
        compiler_params=pltpu.CompilerParams(
            collective_id=1, has_side_effects=True, vmem_limit_bytes=56 * 2**20
        ),
    )(problem, enc, cross_rows, self_rows, kv_rows, cache, perm_cross, perm_self)


def body(
    enc_hidden,
    enc_gain,
    cross_weight,
    assign,
    token_ids,
    cross_table,
    self_table,
    kv_table,
    self_cache,
):
    wide = lax.axis_size("wide")
    narrow = lax.axis_size("narrow")
    me = lax.axis_index("wide")
    side = lax.axis_index("narrow")
    hidden = enc_hidden.astype(jnp.float32)
    squares = jnp.sum(hidden * hidden, axis=1, keepdims=True)
    scaled = (hidden * enc_gain).astype(jnp.bfloat16)
    proj = jnp.dot(scaled, cross_weight, preferred_element_type=jnp.float32)
    part = jnp.concatenate([proj, jnp.broadcast_to(squares, (proj.shape[0], 128))], axis=1)

    steps, cand = token_ids.shape[1:]
    rows = steps * cand
    own = cand // narrow
    flat = token_ids.reshape(1, rows)
    all_ids, parts = exchange(jnp.broadcast_to(flat, (8, rows)), part, wide, narrow)
    summed = part + jnp.sum(parts, axis=0)
    enc = summed[:, : 2 * HEAD] * lax.rsqrt(summed[:, 2 * HEAD :][:, :1] / D + EPS)
    enc = enc.astype(jnp.bfloat16)

    per_owner = cross_table.shape[0]
    capacity = max(TILE_ROWS, 2 * rows // wide)
    slot = jnp.arange(capacity, dtype=jnp.int32)
    local = all_ids[:, 0, :] - me * per_owner
    mine = (local >= 0) & (local < per_owner)
    count = mine.astype(jnp.int32)
    rank = jnp.cumsum(count, axis=1) - count
    match = mine[:, None, :] & (rank[:, None, :] == slot[None, :, None])
    request = jnp.max(jnp.where(match, local[:, None, :], -1), axis=2).reshape(-1)
    picked = (request[:, None] == jnp.arange(per_owner, dtype=jnp.int32)[None, :]).astype(
        jnp.bfloat16
    )

    def lookup(table):
        return jnp.dot(picked, table, preferred_element_type=jnp.float32).astype(jnp.bfloat16)

    owner = flat[0] // per_owner
    hits = (owner[:, None] == jnp.arange(wide, dtype=jnp.int32)[None, :]).astype(jnp.int32)
    earlier = jnp.cumsum(hits, axis=0) - hits
    target = owner * capacity + jnp.sum(earlier * hits, axis=1)
    perm = (
        target[:, None] == jnp.arange(wide * capacity, dtype=jnp.int32)[None, :]
    ).astype(jnp.bfloat16)
    perm_self = lax.dynamic_slice_in_dim(
        perm.reshape(steps, cand, wide * capacity), side * own, own, 1
    ).reshape(steps * own, wide * capacity)

    problems = wide * enc_hidden.shape[0] // ENC_LEN
    chunks = 2
    dims = (wide, narrow, steps, own, problems, chunks)
    cross, selfs = attend(
        assign,
        enc,
        lookup(cross_table),
        lookup(self_table),
        lookup(kv_table),
        self_cache[0],
        perm,
        perm_self,
        dims,
    )
    return (
        cross.reshape(1, steps, cand, cross.shape[1]),
        selfs.reshape(1, steps, own, HEADS * HEAD),
    )


def solution(mesh):
    placed = (
        P("wide", "narrow"),
        P("narrow"),
        P("narrow", None),
        P("wide"),
        P("wide", None, None),
        P("wide", "narrow"),
        P("wide", "narrow"),
        P("wide", None),
        P("wide", "narrow", None, None),
    )
    return jax.shard_map(
        body,
        mesh=mesh,
        in_specs=placed,
        out_specs=(P("wide", None, None, "narrow"), P("wide", None, "narrow", None)),
        check_vma=False,
    )
```

time: 218 us -> 163 us (0.75)
  Pallas kernels: 0 us -> 138 us
  blocking collectives: 60.6 us -> 0 us
  waiting for transfers between devices: 46 us -> 0 us
  local copies, waits for them, and re-layouts: 29.5 us -> 5.95 us
  matrix products: 31.8 us -> 8.69 us
  between operations: 15 us -> 1.53 us
  other arithmetic: 21.3 us -> 8.21 us
  starting transfers between devices: 12.5 us -> 0 us
    pallas_call x0 -> x2, Pallas kernels: none -> 138 us  [the longest x1 121 us: attend(): pl.pallas_call(functools.partial(main_kernel, dims), out_shape=(jax.Shape...]
    all_to_all x2 -> x0, blocking collectives: 55.6 us -> none  [the longest x1 42 us: body(): lax.all_to_all(lookup(cross_table), 'wide', split_axis=0, concat_axis=0,...]
    all_gather x1 -> x0, waiting for transfers between devices: 26.5 us -> none  [body(): gathered = lax.all_gather(enc_kv, 'wide', axis=0, tiled=True)]
    dot_general x7 -> x4, matrix products: 31.8 us -> 8.69 us  [the longest x3 6.43 us: lookup(): jnp.dot(picked, table, preferred_element_type=jnp.float32)]
    psum x1 -> x0, waiting for transfers between devices: 19.5 us -> none  [body(): projected, squares = lax.psum((part_proj, part_squares), 'narrow')]
    gather x6 -> x0, local copies, waits for them, and re-layouts: 17.6 us -> none  [the longest x3 11.3 us: lookup(): rows = jnp.take(table, index, axis=0)]
    all_to_all x3 -> x0, starting transfers between devices: 12.4 us -> none  [the longest x1 5.2 us: body(): lax.all_to_all(lookup(self_table), 'wide', split_axis=0, concat_axis=0, t...]
    reduce_sum x6 -> x2, other arithmetic: 12.7 us -> 1.76 us  [the longest x1 1.58 us: body(): squares = jnp.sum(hidden * hidden, axis=1, keepdims=True)]
  transfers between devices with their start and end apart: 5 -> 0, of which waited for: 2 -> 0; matrix products, arithmetic and copies ran while one was open for 26% -> 0% of each run, Pallas kernels for 0% -> 0%
where the time goes in v1:
time: 163 us; the launch traced here: 162 us
  Pallas kernels  138 us (85%)
  matrix products  8.69 us (5%)
  other arithmetic  8.21 us (5%)
  local copies, waits for them, and re-layouts  5.95 us (4%)
    pallas_call x1, Pallas kernels, attend(): pl.pallas_call(functools.partial(main_kernel, dims), out_shape=(jax.Shape...  121 us
    pallas_call x1, Pallas kernels, exchange(): pl.pallas_call(functools.partial(exchange_kernel, wide, narrow), out_shap...  16.8 us
    dot_general x3, matrix products, lookup(): jnp.dot(picked, table, preferred_element_type=jnp.float32)  6.43 us
    unnamed x7, local copies, waits for them, and re-layouts  4.14 us

profile of v1, /device:TPU:0, one launch (start us, length us, event | category | flops | bytes accessed | tf_op | source)
XLA Modules:
  0.0 162.1 jit_solution(8869560336609968534)
XLA Ops:
  0.6 0.0 copy-start
  1.4 0.9 broadcast_in_dim.21
  2.4 1.6 fusion.1
  3.9 0.6 broadcast_in_dim.22.ids_ref
  4.5 0.1 fusion.14
  4.6 0.2 reduce_window_sum.23
  4.8 0.2 select_reduce_fusion.1
  5.0 0.1 reduce_sum.29
  5.1 0.7 multiply_add_fusion
  5.8 0.1 constant_dynamic-slice_fusion
  5.9 0.7 fusion.15
  6.5 0.7 fusion.10.perm_cross_ref
  7.2 0.1 broadcast_in_dim.20
  7.3 2.3 %fusion.2 = f32[192,256]{1,0:T(8,128)S(1)} fusion(bf16[3072,256]{1,0:T(8,128)(2,1)} %param.11, bf16[192,3072]{1,0:T(8,128)(2,1)} %param.9, f32[3072]{0:T(1024)} %param.10), kind=kOutput, calls=%fused_computation.6 | convolution fusion | flops 303759360 | bytes 2961408 | tf_op jit(solution)/shard_map/dot_general | solution.py:452
  9.6 0.7 pad_maximum_fusion.part_ref
  10.3 16.8 %shard_map.104 = (s32[16,8,128]{2,1,0:T(8,128)}, f32[1,192,384]{2,1,0:T(8,128)}) custom-call(s32[8,128]{1,0:T(8,128)} %broadcast_in_dim.22.ids_ref, f32[192,384]{1,0:T(8,128)} %pad_maximum_fusion.part_ref), custom_call_target="tpu_custom_call" | custom-call | tf_op jit(solution)/shard_map/pallas_call | solution.py:89
  27.2 1.0 bitcast_add_fusion
  28.2 0.1 fusion.13
  28.3 0.7 fusion.8.enc_ref
  29.0 0.9 fusion.16
  29.9 0.3 reduce_window_sum.22
  30.2 0.3 select_reduce_fusion
  30.6 0.1 eq.67
  30.7 1.9 %convolution_convert_fusion.2.kv_ref = bf16[256,256]{1,0:T(8,128)(2,1)} fusion(bf16[500,256]{1,0:T(8,128)(2,1)} %param.16, s32[256]{0:T(256)S(1)} %eq.67), kind=kOutput, calls=%fused_computation.8 | convolution fusion | flops 65729536 | bytes 388096 | tf_op jit(solution)/shard_map/dot_general | solution.py:478
  32.5 0.0 copy-done
  32.5 0.0 copy-start.1
  32.5 2.2 %convolution_convert_fusion.self_ref = bf16[256,3072]{1,0:T(8,128)(2,1)} fusion(bf16[500,3072]{1,0:T(8,128)(2,1)S(1)} %copy-done, s32[256]{0:T(256)S(1)} %eq.67), kind=kOutput, calls=%fused_computation | convolution fusion | flops 787346432 | bytes 4645888 | tf_op jit(solution)/shard_map/dot_general | solution.py:478
  34.8 0.0 copy-done.1
  34.8 2.3 %convolution_convert_fusion.1.cross_ref = bf16[256,3072]{1,0:T(8,128)(2,1)} fusion(bf16[500,3072]{1,0:T(8,128)(2,1)S(1)} %copy-done.1, s32[256]{0:T(256)S(1)} %eq.67), kind=kOutput, calls=%fused_computation.1 | convolution fusion | flops 787346432 | bytes 4645888 | tf_op jit(solution)/shard_map/dot_general | solution.py:478
  37.1 120.8 %shard_map.105 = (bf16[128,3072]{1,0:T(8,128)(2,1)}, bf16[64,6144]{1,0:T(8,128)(2,1)}) custom-call(s32[1]{0:T(128)S(6)} %copy.22.problem_ref, bf16[192,256]{1,0:T(8,128)(2,1)} %fusion.8.enc_ref, bf16[256,3072]{1,0:T(8,128)(2,1)} %convolution_convert_fusion.1.cross_ref, bf16[256,3072]{1,0:T(8,128)(2,1)} %convolution_convert_fusion.self_ref, ...), custom_call_target="tpu_custom_call" | custom-call | tf_op jit(solution)/shard_map/pallas_call | solution.py:389
  157.9 2.1 %copy.23 = bf16[1,2,64,3072]{3,2,1,0:T(8,128)(2,1)} copy(bf16[1,2,64,3072]{3,2,1,0:T(8,128)(2,1)} %bitcast.27) | data formatting | bytes 1572864
  160.0 2.1 %copy.24 = bf16[1,2,32,6144]{3,2,1,0:T(8,128)(2,1)} copy(bf16[1,2,32,6144]{3,2,1,0:T(8,128)(2,1)} %bitcast.26) | data formatting | bytes 1572864
  (4 shorter events, 0.1 us)
Async XLA Ops:
  0.6 31.9 %copy-start = (bf16[500,3072]{1,0:T(8,128)(2,1)S(1)}, bf16[500,3072]{1,0:T(8,128)(2,1)}, u32[]{:S(2)}) copy-start(bf16[500,3072]{1,0:T(8,128)(2,1)} %param.15) | copy-start | bytes 9216004
  32.5 2.2 %copy-start.1 = (bf16[500,3072]{1,0:T(8,128)(2,1)S(1)}, bf16[500,3072]{1,0:T(8,128)(2,1)}, u32[]{:S(2)}) copy-start(bf16[500,3072]{1,0:T(8,128)(2,1)} %param.14) | copy-start | bytes 9216004

commit v2 on v1

--- a/solution.py
+++ b/solution.py
@@ -20,6 +20,10 @@
 DOT_T = (((1,), (1,)), ((), ()))
 
 
+def most_parts(count, limit=4):
+    return max(parts for parts in range(1, limit + 1) if count % parts == 0)
+
+
 def greet(wide, narrow):
     me = lax.axis_index("wide")
     side = lax.axis_index("narrow")
@@ -41,81 +45,87 @@
     pl.semaphore_wait(barrier, wide + narrow - 2)
 
 
-def exchange_kernel(
-    wide, narrow, ids_ref, part_ref, ids_out, parts_out, id_send, id_recv, part_send, part_recv
-):
+def pick_kernel(wide, per_owner, capacity, ids_ref, picked_out, all_ids, id_send, id_recv):
     me = lax.axis_index("wide")
-    side = lax.axis_index("narrow")
-    greet(wide, narrow)
+    greet(wide, 1)
 
     def ids_copy(step):
         return pltpu.make_async_remote_copy(
             src_ref=ids_ref,
-            dst_ref=ids_out.at[me],
+            dst_ref=all_ids.at[me],
             send_sem=id_send.at[step],
             recv_sem=id_recv.at[step],
             device_id={"wide": lax.rem(me + step, wide)},
             device_id_type=MESH_ID,
         )
 
-    def part_copy(step):
-        return pltpu.make_async_remote_copy(
-            src_ref=part_ref,
-            dst_ref=parts_out.at[step - 1],
-            send_sem=part_send.at[step],
-            recv_sem=part_recv.at[step],
-            device_id={"narrow": lax.rem(side + step, narrow)},
-            device_id_type=MESH_ID,
-        )
-
     @pl.loop(1, wide)
     def _(step):
         ids_copy(step).start()
 
-    for step in range(1, narrow):
-        part_copy(step).start()
-    ids_out[me] = ids_ref[...]
+    all_ids[me] = ids_ref[...]
+    rows = ids_ref.shape[1]
+    before = lax.broadcasted_iota(jnp.int32, (rows, rows), 0)
+    after = lax.broadcasted_iota(jnp.int32, (rows, rows), 1)
+    earlier = jnp.where(before < after, 1.0, 0.0).astype(jnp.bfloat16)
+    slot = lax.broadcasted_iota(jnp.int32, (capacity, rows), 0).astype(jnp.float32)
+    entry = lax.broadcasted_iota(jnp.int32, (capacity, per_owner), 1).astype(jnp.float32)
 
     @pl.loop(1, wide)
     def _(step):
         ids_copy(step).wait()
 
-    for step in range(1, narrow):
-        part_copy(step).wait()
-
-
-def exchange(ids, part, wide, narrow):
+    for group in range(wide):
+        local = all_ids[group] - me * per_owner
+        mine = jnp.where((local >= 0) & (local < per_owner), 1.0, 0.0)
+        rank = jnp.dot(mine.astype(jnp.bfloat16), earlier, preferred_element_type=jnp.float32)
+        key = jnp.where(mine > 0.0, rank, -1.0)[:1]
+        request = jnp.max(
+            jnp.where(slot == key, local[:1].astype(jnp.float32), -1.0), axis=1, keepdims=True
+        )
+        picked_out[group * capacity : (group + 1) * capacity, :] = jnp.where(
+            entry == request, 1.0, 0.0
+        ).astype(jnp.bfloat16)
+
+
+def pick(ids, per_owner, capacity, wide):
     vmem = pl.BlockSpec(memory_space=pltpu.VMEM)
     return pl.pallas_call(
-        functools.partial(exchange_kernel, wide, narrow),
-        out_shape=(
-            jax.ShapeDtypeStruct((wide,) + ids.shape, ids.dtype),
-            jax.ShapeDtypeStruct((narrow - 1,) + part.shape, part.dtype),
-        ),
-        in_specs=[vmem, vmem],
-        out_specs=(vmem, vmem),
+        functools.partial(pick_kernel, wide, per_owner, capacity),
+        out_shape=jax.ShapeDtypeStruct((wide * capacity, per_owner), jnp.bfloat16),
+        in_specs=[vmem],
+        out_specs=vmem,
         scratch_shapes=[
+            pltpu.VMEM((wide,) + ids.shape, ids.dtype),
             pltpu.SemaphoreType.DMA((wide,)),
             pltpu.SemaphoreType.DMA((wide,)),
-            pltpu.SemaphoreType.DMA((narrow,)),
-            pltpu.SemaphoreType.DMA((narrow,)),
         ],
         compiler_params=pltpu.CompilerParams(collective_id=0, has_side_effects=True),
-    )(ids, part)
+    )(ids)
 
 
 def main_kernel(
     dims,
     problem_ref,
-    enc_ref,
-    cross_ref,
+    ids_ref,
+    hidden_ref,
+    gain_ref,
+    weight_ref,
+    picked_ref,
+    table_ref,
     self_ref,
     kv_ref,
     cache_ref,
+    cross_out,
+    self_out,
+    hidden,
+    weight,
+    table,
+    part,
+    parts,
+    cross_ref,
     perm_cross_ref,
     perm_self_ref,
-    cross_out,
-    self_out,
     enc_buf,
     keys,
     cross_raw,
@@ -126,6 +136,8 @@
     q_rows,
     o_rows,
     local_sem,
+    part_send,
+    part_recv,
     enc_send,
     enc_recv,
     self_send,
@@ -141,8 +153,9 @@
     me = lax.axis_index("wide")
     side = lax.axis_index("narrow")
     levels = wide.bit_length() - 1
-    enc_rows = enc_ref.shape[0]
+    enc_rows = hidden_ref.shape[0]
     features = cross_ref.shape[1]
+    kv_cols = kv_ref.shape[1]
     heads_dev = features // HEAD
     chunk_cols = features // chunks
     cap = cross_ref.shape[0] // wide
@@ -208,63 +221,119 @@
             device_id_type=MESH_ID,
         )
 
+    def part_copy(hop):
+        return pltpu.make_async_remote_copy(
+            src_ref=part,
+            dst_ref=parts.at[hop - 1],
+            send_sem=part_send.at[hop - 1],
+            recv_sem=part_recv.at[hop - 1],
+            device_id={"narrow": lax.rem(side + hop, narrow)},
+            device_id_type=MESH_ID,
+        )
+
     own_block = rows_of(me)
     locals_ = [
-        pltpu.make_async_copy(
-            enc_ref,
-            enc_buf.at[pl.ds(pl.multiple_of(place * enc_rows, enc_rows), enc_rows)],
-            local_sem.at[0],
-        ),
+        pltpu.make_async_copy(hidden_ref, hidden, local_sem.at[0]),
         pltpu.make_async_copy(
             self_ref.at[own_block], self_raw.at[side, own_block], local_sem.at[1]
         ),
         pltpu.make_async_copy(kv_ref.at[own_block], kv_raw.at[own_block], local_sem.at[2]),
-        pltpu.make_async_copy(cross_ref.at[own_block], cross_raw.at[own_block], local_sem.at[3]),
-        pltpu.make_async_copy(cache_ref, cache, local_sem.at[4]),
+        pltpu.make_async_copy(weight_ref, weight, local_sem.at[3]),
+        pltpu.make_async_copy(table_ref, table, local_sem.at[4]),
+        pltpu.make_async_copy(cache_ref, cache, local_sem.at[5]),
     ]
     for copy in locals_:
         copy.start()
     greet(wide, narrow)
-    locals_[0].wait()
-    enc_copy(0).start()
 
     @pl.loop(1, wide)
     def _(step):
         kv_copy(step).start()
-
-    bounds = [1 + (wide - 1) * level // levels for level in range(levels + 1)]
-    for level in range(levels):
-
-        @pl.loop(bounds[level], bounds[level + 1])
-        def _(step):
-            self_copy(step).start()
-
-        enc_copy(level).wait()
-        if level + 1 < levels:
-            enc_copy(level + 1).start()
+        self_copy(step).start()
 
     locals_[1].wait()
     for hop in range(1, narrow):
         side_copy(0, hop).start()
 
-    @pl.loop(1, wide)
-    def _(step):
+    locals_[0].wait()
+    locals_[3].wait()
+    part[...] = jnp.zeros_like(part)
+    depth = 256
+
+    @pl.loop(0, hidden.shape[1] // depth)
+    def _(index):
+        span = pl.ds(pl.multiple_of(index * depth, depth), depth)
+        values = hidden[:, span].astype(jnp.float32)
+        scaled = (values * gain_ref[:, span]).astype(jnp.bfloat16)
+        part[:, :kv_cols] += jnp.dot(scaled, weight[span, :], preferred_element_type=jnp.float32)
+        squares = values * values
+        part[:, kv_cols:] += sum(
+            squares[:, lane : lane + HEAD] for lane in range(0, depth, HEAD)
+        )
+
+    locals_[4].wait()
+
+    @pl.loop(0, features // 256)
+    def _(index):
+        cols = pl.ds(pl.multiple_of(index * 256, 256), 256)
+        cross_ref[:, cols] = jnp.dot(
+            picked_ref[...], table[:, cols], preferred_element_type=jnp.float32
+        ).astype(jnp.bfloat16)
+
+    for hop in range(1, narrow):
+        part_copy(hop).start()
+
+    rows_total = ids_ref.shape[1]
+    per_owner = table_ref.shape[0]
+    ids = ids_ref[:1, :]
+    owner = jnp.zeros_like(ids)
+    for device in range(1, wide):
+        owner = owner + jnp.where(ids >= device * per_owner, 1, 0)
+    across = jnp.broadcast_to(owner.astype(jnp.float32), (rows_total, rows_total))
+    down = jnp.transpose(across)
+    row = lax.broadcasted_iota(jnp.int32, (rows_total, rows_total), 0)
+    col = lax.broadcasted_iota(jnp.int32, (rows_total, rows_total), 1)
+    rank = jnp.sum(jnp.where((across == down) & (col < row), 1.0, 0.0), axis=1, keepdims=True)
+    target = down[:, :1] * cap + rank
+    place_of = lax.broadcasted_iota(jnp.int32, perm_cross_ref.shape, 1).astype(jnp.float32)
+    perm_cross_ref[...] = jnp.where(place_of == target, 1.0, 0.0).astype(jnp.bfloat16)
+    cand = rows_total // steps
+    for step in range(steps):
+        mine = pl.ds(pl.multiple_of(step * cand + side * own, own), own)
+        perm_self_ref[step * own : (step + 1) * own, :] = perm_cross_ref[mine, :]
+
+    def pass_on(step):
         self_copy(step).wait_recv()
         for hop in range(1, narrow):
             side_copy(step, hop).start()
-        for chunk in range(chunks):
+        cross_copy(step, 0).start()
+
+    early = 1 + (wide - 1) // 4
+    pl.loop(1, early)(pass_on)
+
+    for hop in range(1, narrow):
+        part_copy(hop).wait()
+    summed = part[...]
+    for hop in range(1, narrow):
+        summed = summed + parts[hop - 1]
+    squares = jnp.sum(summed[:, kv_cols:], axis=1, keepdims=True)
+    enc_buf[pl.ds(pl.multiple_of(place * enc_rows, enc_rows), enc_rows), :] = (
+        summed[:, :kv_cols] * lax.rsqrt(squares / D + EPS)
+    ).astype(jnp.bfloat16)
+
+    pl.loop(early, early + 1)(pass_on)
+    enc_copy(0).start()
+    pl.loop(early + 1, wide)(pass_on)
+    cross_raw[own_block, :] = cross_ref[own_block, :]
+
+    for level in range(levels - 2):
+        enc_copy(level).wait()
+        enc_copy(level + 1).start()
+    for chunk in range(1, chunks):
+
+        @pl.loop(1, wide)
+        def _(step):
             cross_copy(step, chunk).start()
-
-    problem = problem_ref[0]
-    problem_bits = problems.bit_length() - 1
-    for block in range(wide // problems):
-        mine = None
-        for other in range(problems):
-            turned = sum((other >> bit) % 2 << (problem_bits - 1 - bit) for bit in range(problem_bits))
-            start = (block * problems + turned) * enc_rows
-            rows = enc_buf[start : start + enc_rows, :]
-            mine = rows if mine is None else jnp.where(problem == other, rows, mine)
-        keys[block * enc_rows : (block + 1) * enc_rows, :] = mine
 
     locals_[2].wait()
 
@@ -280,21 +349,20 @@
             side_copy(step, hop).wait()
 
     total_rows = steps * own
-    for part in range(narrow):
+    for other in range(narrow):
 
         @pl.loop(0, heads_dev)
         def _(head):
             cols = pl.ds(pl.multiple_of(head * HEAD, HEAD), HEAD)
             moved = jnp.dot(
-                perm_self_ref[...], self_raw[part, :, cols], preferred_element_type=jnp.float32
+                perm_self_ref[...], self_raw[other, :, cols], preferred_element_type=jnp.float32
             )
-            start = pl.multiple_of((part * heads_dev + head) * total_rows, total_rows)
+            start = pl.multiple_of((other * heads_dev + head) * total_rows, total_rows)
             q_rows[pl.ds(start, total_rows), :] = moved
 
-    locals_[4].wait()
-
-    @pl.loop(0, own, unroll=2)
-    def _(cand):
+    locals_[5].wait()
+
+    def attend_one(cand):
         rows = [
             q_rows[pl.ds(step * own + cand, HEADS, stride=total_rows), :] for step in range(steps)
         ]
@@ -329,15 +397,30 @@
                 step * HEADS : (step + 1) * HEADS
             ]
 
+    enc_copy(levels - 2).wait()
+    enc_copy(levels - 1).start()
+    pl.loop(0, own, unroll=2)(attend_one)
+    enc_copy(levels - 1).wait()
+
     @pl.loop(0, HEADS)
     def _(head):
         start = pl.multiple_of(head * total_rows, total_rows)
         cols = pl.ds(pl.multiple_of(head * HEAD, HEAD), HEAD)
         self_out[:, cols] = o_rows[pl.ds(start, total_rows), :].astype(jnp.bfloat16)
 
-    locals_[3].wait()
+    problem = problem_ref[0]
+    problem_bits = problems.bit_length() - 1
+    for block in range(wide // problems):
+        mine = None
+        for other in range(problems):
+            turned = sum((other >> bit) % 2 << (problem_bits - 1 - bit) for bit in range(problem_bits))
+            start = (block * problems + turned) * enc_rows
+            rows = enc_buf[start : start + enc_rows, :]
+            mine = rows if mine is None else jnp.where(problem == other, rows, mine)
+        keys[block * enc_rows : (block + 1) * enc_rows, :] = mine
+
     query_rows = perm_cross_ref.shape[0]
-    group = math.gcd(heads_dev // chunks, 4)
+    group = most_parts(heads_dev // chunks)
     for chunk in range(chunks):
 
         @pl.loop(1, wide)
@@ -376,34 +459,46 @@
             cross_copy(step, chunk).wait_send()
 
 
-def attend(problem, enc, cross_rows, self_rows, kv_rows, cache, perm_cross, perm_self, dims):
+def attend(problem, ids, hidden, gain, weight, picked, table, self_rows, kv_rows, cache, dims):
     wide, narrow, steps, own, problems, chunks = dims
-    slots, features = cross_rows.shape
-    enc_rows, kv_cols = enc.shape
+    slots, features = self_rows.shape
+    enc_rows = hidden.shape[0]
+    kv_cols = kv_rows.shape[1]
     levels = wide.bit_length() - 1
     vmem = pl.BlockSpec(memory_space=pltpu.VMEM)
     anywhere = pl.BlockSpec(memory_space=pl.ANY)
     total_rows = steps * own
     bf16 = jnp.bfloat16
     dma = pltpu.SemaphoreType.DMA
+    part = (enc_rows, kv_cols + HEAD)
     return pl.pallas_call(
         functools.partial(main_kernel, dims),
         out_shape=(
-            jax.ShapeDtypeStruct((perm_cross.shape[0], features), bf16),
+            jax.ShapeDtypeStruct((ids.shape[1], features), bf16),
             jax.ShapeDtypeStruct((total_rows, HEADS * HEAD), bf16),
         ),
         in_specs=[
             pl.BlockSpec(memory_space=pltpu.SMEM),
+            vmem,
+            anywhere,
+            vmem,
+            anywhere,
+            vmem,
             anywhere,
             anywhere,
             anywhere,
             anywhere,
-            anywhere,
-            vmem,
-            vmem,
         ],
         out_specs=(vmem, vmem),
         scratch_shapes=[
+            pltpu.VMEM(hidden.shape, bf16),
+            pltpu.VMEM(weight.shape, bf16),
+            pltpu.VMEM(table.shape, bf16),
+            pltpu.VMEM(part, jnp.float32),
+            pltpu.VMEM((narrow - 1,) + part, jnp.float32),
+            pltpu.VMEM((slots, features), bf16),
+            pltpu.VMEM((ids.shape[1], slots), bf16),
+            pltpu.VMEM((total_rows, slots), bf16),
             pltpu.VMEM((wide * enc_rows, kv_cols), bf16),
             pltpu.VMEM((wide // problems * enc_rows, kv_cols), bf16),
             pltpu.VMEM((slots, features), bf16),
@@ -413,7 +508,9 @@
             pltpu.VMEM((total_rows, kv_cols), jnp.float32),
             pltpu.VMEM((HEADS * total_rows, HEAD), jnp.float32),
             pltpu.VMEM((HEADS * total_rows, HEAD), jnp.float32),
-            dma((5,)),
+            dma((6,)),
+            dma((narrow - 1,)),
+            dma((narrow - 1,)),
             dma((levels,)),
             dma((levels,)),
             dma((wide,)),
@@ -428,7 +525,7 @@
         compiler_params=pltpu.CompilerParams(
             collective_id=1, has_side_effects=True, vmem_limit_bytes=56 * 2**20
         ),
-    )(problem, enc, cross_rows, self_rows, kv_rows, cache, perm_cross, perm_self)
+    )(problem, ids, hidden, gain, weight, picked, table, self_rows, kv_rows, cache)
 
 
 def body(
@@ -444,63 +541,31 @@
 ):
     wide = lax.axis_size("wide")
     narrow = lax.axis_size("narrow")
-    me = lax.axis_index("wide")
-    side = lax.axis_index("narrow")
-    hidden = enc_hidden.astype(jnp.float32)
-    squares = jnp.sum(hidden * hidden, axis=1, keepdims=True)
-    scaled = (hidden * enc_gain).astype(jnp.bfloat16)
-    proj = jnp.dot(scaled, cross_weight, preferred_element_type=jnp.float32)
-    part = jnp.concatenate([proj, jnp.broadcast_to(squares, (proj.shape[0], 128))], axis=1)
-
     steps, cand = token_ids.shape[1:]
     rows = steps * cand
     own = cand // narrow
-    flat = token_ids.reshape(1, rows)
-    all_ids, parts = exchange(jnp.broadcast_to(flat, (8, rows)), part, wide, narrow)
-    summed = part + jnp.sum(parts, axis=0)
-    enc = summed[:, : 2 * HEAD] * lax.rsqrt(summed[:, 2 * HEAD :][:, :1] / D + EPS)
-    enc = enc.astype(jnp.bfloat16)
-
     per_owner = cross_table.shape[0]
     capacity = max(TILE_ROWS, 2 * rows // wide)
-    slot = jnp.arange(capacity, dtype=jnp.int32)
-    local = all_ids[:, 0, :] - me * per_owner
-    mine = (local >= 0) & (local < per_owner)
-    count = mine.astype(jnp.int32)
-    rank = jnp.cumsum(count, axis=1) - count
-    match = mine[:, None, :] & (rank[:, None, :] == slot[None, :, None])
-    request = jnp.max(jnp.where(match, local[:, None, :], -1), axis=2).reshape(-1)
-    picked = (request[:, None] == jnp.arange(per_owner, dtype=jnp.int32)[None, :]).astype(
-        jnp.bfloat16
-    )
+    ids = jnp.broadcast_to(token_ids.reshape(1, rows), (8, rows))
+    picked = pick(ids, per_owner, capacity, wide)
 
     def lookup(table):
         return jnp.dot(picked, table, preferred_element_type=jnp.float32).astype(jnp.bfloat16)
 
-    owner = flat[0] // per_owner
-    hits = (owner[:, None] == jnp.arange(wide, dtype=jnp.int32)[None, :]).astype(jnp.int32)
-    earlier = jnp.cumsum(hits, axis=0) - hits
-    target = owner * capacity + jnp.sum(earlier * hits, axis=1)
-    perm = (
-        target[:, None] == jnp.arange(wide * capacity, dtype=jnp.int32)[None, :]
-    ).astype(jnp.bfloat16)
-    perm_self = lax.dynamic_slice_in_dim(
-        perm.reshape(steps, cand, wide * capacity), side * own, own, 1
-    ).reshape(steps * own, wide * capacity)
-
     problems = wide * enc_hidden.shape[0] // ENC_LEN
-    chunks = 2
-    dims = (wide, narrow, steps, own, problems, chunks)
+    chunks = most_parts(cross_table.shape[1] // HEAD)
     cross, selfs = attend(
         assign,
-        enc,
-        lookup(cross_table),
+        ids,
+        enc_hidden,
+        enc_gain.reshape(1, -1),
+        cross_weight,
+        picked,
+        cross_table,
         lookup(self_table),
         lookup(kv_table),
         self_cache[0],
-        perm,
-        perm_self,
-        dims,
+        (wide, narrow, steps, own, problems, chunks),
     )
     return (
         cross.reshape(1, steps, cand, cross.shape[1]),

time: 163 us -> 129 us (0.79)
  Pallas kernels: 138 us -> 117 us
  other arithmetic: 8.21 us -> 0 us
  matrix products: 8.69 us -> 5.03 us
    pallas_call x1, Pallas kernels: 121 us -> 106 us  [attend(): pl.pallas_call(functools.partial(main_kernel, dims), out_shape=(jax.Shape...]
    pallas_call x1, Pallas kernels: 16.8 us -> 10.6 us  [pick(): pl.pallas_call(functools.partial(pick_kernel, wide, per_owner, capacity),...]
    convert_element_type x5 -> x0, other arithmetic: 3.06 us -> none  [the longest x2 1.38 us: body(): perm = (target[:, None] == jnp.arange(wide * capacity, dtype=jnp.int32)[N...]
    dot_general x1 -> x0, matrix products: 2.26 us -> none  [body(): proj = jnp.dot(scaled, cross_weight, preferred_element_type=jnp.float32)]
    reduce_sum x2 -> x0, other arithmetic: 1.76 us -> none  [the longest x1 1.58 us: body(): squares = jnp.sum(hidden * hidden, axis=1, keepdims=True)]
    add x3 -> x0, other arithmetic: 1.71 us -> none  [the longest x1 1 us: body(): summed = part + jnp.sum(parts, axis=0)]
    dot_general x3 -> x2, matrix products: 6.43 us -> 5.03 us  [lookup(): jnp.dot(picked, table, preferred_element_type=jnp.float32)]
    unnamed x7 -> x4, local copies, waits for them, and re-layouts: 4.14 us -> 4.14 us
where the time goes in v2:
time: 129 us
  Pallas kernels  117 us (91%)
  local copies, waits for them, and re-layouts  5.63 us (4%)
  matrix products  5.03 us (4%)
  between operations  1.45 us (1%)
    pallas_call x1, Pallas kernels, attend(): pl.pallas_call(functools.partial(main_kernel, dims), out_shape=(jax.Shape...  106 us
    pallas_call x1, Pallas kernels, pick(): pl.pallas_call(functools.partial(pick_kernel, wide, per_owner, capacity),...  10.6 us
    dot_general x2, matrix products, lookup(): jnp.dot(picked, table, preferred_element_type=jnp.float32)  5.03 us
    unnamed x4, local copies, waits for them, and re-layouts  4.14 us

profile of v2, /device:TPU:0, one launch (start us, length us, event | category | flops | bytes accessed | tf_op | source)
XLA Modules:
  0.0 128.9 jit_solution(17762623820540374983)
XLA Ops:
  0.6 0.0 copy-start
  1.4 0.9 broadcast_in_dim.7
  2.3 0.6 broadcast_in_dim.8.ids_ref
  2.9 10.6 %shard_map.104.picked_ref = bf16[256,500]{1,0:T(8,128)(2,1)} custom-call(s32[8,128]{1,0:T(8,128)} %broadcast_in_dim.8.ids_ref), custom_call_target="tpu_custom_call" | custom-call | tf_op jit(solution)/shard_map/pallas_call | solution.py:93
  13.6 1.9 %convolution_convert_fusion.1.kv_ref = bf16[256,256]{1,0:T(8,128)(2,1)} fusion(bf16[256,500]{1,0:T(8,128)(2,1)} %shard_map.104.picked_ref, bf16[500,256]{1,0:T(8,128)(2,1)} %param.16), kind=kOutput, calls=%fused_computation.1 | convolution fusion | flops 65601536 | bytes 643072 | tf_op jit(solution)/shard_map/dot_general | solution.py:553
  15.5 0.0 copy-done
  15.5 3.1 %convolution_convert_fusion.self_ref = bf16[256,3072]{1,0:T(8,128)(2,1)} fusion(bf16[256,500]{1,0:T(8,128)(2,1)} %shard_map.104.picked_ref, bf16[500,3072]{1,0:T(8,128)(2,1)S(1)} %copy-done), kind=kOutput, calls=%fused_computation | convolution fusion | flops 787218432 | bytes 4900864 | tf_op jit(solution)/shard_map/dot_general | solution.py:553
  18.6 106.1 %shard_map.105 = (bf16[128,3072]{1,0:T(8,128)(2,1)}, bf16[64,6144]{1,0:T(8,128)(2,1)}) custom-call(s32[1]{0:T(128)S(6)} %copy.13.problem_ref, s32[8,128]{1,0:T(8,128)} %broadcast_in_dim.8.ids_ref, bf16[192,3072]{1,0:T(8,128)(2,1)} %hidden_ref.1, f32[1,3072]{1,0:T(1,128)} %bitcast.11, bf16[3072,256]{1,0:T(8,128)(2,1)} %weight_ref.1, ...), custom_call_target="tpu_custom_call" | custom-call | tf_op jit(solution)/shard_map/pallas_call | solution.py:474
  124.7 2.1 %copy.14 = bf16[1,2,64,3072]{3,2,1,0:T(8,128)(2,1)} copy(bf16[1,2,64,3072]{3,2,1,0:T(8,128)(2,1)} %bitcast.10) | data formatting | bytes 1572864
  126.8 2.1 %copy.15 = bf16[1,2,32,6144]{3,2,1,0:T(8,128)(2,1)} copy(bf16[1,2,32,6144]{3,2,1,0:T(8,128)(2,1)} %bitcast.9) | data formatting | bytes 1572864
Async XLA Ops:
  0.6 14.8 %copy-start = (bf16[500,3072]{1,0:T(8,128)(2,1)S(1)}, bf16[500,3072]{1,0:T(8,128)(2,1)}, u32[]{:S(2)}) copy-start(bf16[500,3072]{1,0:T(8,128)(2,1)} %param.15) | copy-start | bytes 9216004

commit v3 on v2

--- a/solution.py
+++ b/solution.py
@@ -246,10 +246,18 @@
         copy.start()
     greet(wide, narrow)
 
+    window = min(6, wide - 1)
+
+    def turn(index):
+        return lax.rem(index + wide // 2 - 2, wide - 1) + 1
+
+    @pl.loop(1, 1 + window)
+    def _(index):
+        self_copy(turn(index)).start()
+
     @pl.loop(1, wide)
     def _(step):
         kv_copy(step).start()
-        self_copy(step).start()
 
     locals_[1].wait()
     for hop in range(1, narrow):
@@ -302,14 +310,29 @@
         mine = pl.ds(pl.multiple_of(step * cand + side * own, own), own)
         perm_self_ref[step * own : (step + 1) * own, :] = perm_cross_ref[mine, :]
 
-    def pass_on(step):
+    def pass_on(index):
+        step = turn(index)
         self_copy(step).wait_recv()
         for hop in range(1, narrow):
             side_copy(step, hop).start()
-        cross_copy(step, 0).start()
-
-    early = 1 + (wide - 1) // 4
-    pl.loop(1, early)(pass_on)
+
+    def pass_and_self(index):
+        pass_on(index)
+        self_copy(turn(index + window)).start()
+
+    def pass_and_cross(index):
+        pass_on(index)
+        cross_copy(turn(index - (wide - 1 - window)), 0).start()
+
+    def advance(first, last):
+        middle = min(max(first, wide - window), last)
+        if first < middle:
+            pl.loop(first, middle)(pass_and_self)
+        if middle < last:
+            pl.loop(middle, last)(pass_and_cross)
+
+    marks = [1 + (wide - 1) * k // 15 for k in (4, 5, 9, 13)]
+    advance(1, marks[0])
 
     for hop in range(1, narrow):
         part_copy(hop).wait()
@@ -321,19 +344,28 @@
         summed[:, :kv_cols] * lax.rsqrt(squares / D + EPS)
     ).astype(jnp.bfloat16)
 
-    pl.loop(early, early + 1)(pass_on)
+    advance(marks[0], marks[1])
     enc_copy(0).start()
-    pl.loop(early + 1, wide)(pass_on)
+    for level in (1, 2):
+        advance(marks[level], marks[level + 1])
+        if level < levels - 1:
+            enc_copy(level - 1).wait()
+            enc_copy(level).start()
+    advance(marks[3], wide)
     cross_raw[own_block, :] = cross_ref[own_block, :]
-
-    for level in range(levels - 2):
-        enc_copy(level).wait()
-        enc_copy(level + 1).start()
+    for level in range(3, levels - 1):
+        enc_copy(level - 1).wait()
+        enc_copy(level).start()
+
+    @pl.loop(1 + window, wide)
+    def _(index):
+        cross_copy(turn(index), 0).start()
+
     for chunk in range(1, chunks):
 
         @pl.loop(1, wide)
-        def _(step):
-            cross_copy(step, chunk).start()
+        def _(index):
+            cross_copy(turn(index), chunk).start()
 
     locals_[2].wait()
 
@@ -397,9 +429,10 @@
                 step * HEADS : (step + 1) * HEADS
             ]
 
+    pl.loop(0, own // 2, unroll=2)(attend_one)
     enc_copy(levels - 2).wait()
     enc_copy(levels - 1).start()
-    pl.loop(0, own, unroll=2)(attend_one)
+    pl.loop(own // 2, own, unroll=2)(attend_one)
     enc_copy(levels - 1).wait()
 
     @pl.loop(0, HEADS)
@@ -528,6 +561,32 @@
     )(problem, ids, hidden, gain, weight, picked, table, self_rows, kv_rows, cache)
 
 
+def hand_over_kernel(count, *refs):
+    ins, outs, holds, sems = refs[:count], refs[count : 2 * count], refs[2 * count : -1], refs[-1]
+    loads = [pltpu.make_async_copy(ins[k], holds[k], sems.at[0, k]) for k in range(count)]
+    stores = [pltpu.make_async_copy(holds[k], outs[k], sems.at[1, k]) for k in range(count)]
+    for copy in loads:
+        copy.start()
+    for load, store in zip(loads, stores):
+        load.wait()
+        store.start()
+    for copy in stores:
+        copy.wait()
+
+
+def hand_over(arrays):
+    count = len(arrays)
+    anywhere = pl.BlockSpec(memory_space=pl.ANY)
+    return pl.pallas_call(
+        functools.partial(hand_over_kernel, count),
+        out_shape=tuple(jax.ShapeDtypeStruct(array.shape, array.dtype) for array in arrays),
+        in_specs=[anywhere] * count,
+        out_specs=(anywhere,) * count,
+        scratch_shapes=[pltpu.VMEM(array.shape, array.dtype) for array in arrays]
+        + [pltpu.SemaphoreType.DMA((2, count))],
+    )(*arrays)
+
+
 def body(
     enc_hidden,
     enc_gain,
@@ -567,6 +626,7 @@
         self_cache[0],
         (wide, narrow, steps, own, problems, chunks),
     )
+    cross, selfs = hand_over([cross, selfs])
     return (
         cross.reshape(1, steps, cand, cross.shape[1]),
         selfs.reshape(1, steps, own, HEADS * HEAD),

time: 129 us -> 120 us (0.930)
  Pallas kernels: 117 us -> 112 us
  local copies, waits for them, and re-layouts: 5.63 us -> 1.51 us
    pallas_call x1, Pallas kernels: 106 us -> 99.1 us  [attend(): pl.pallas_call(functools.partial(main_kernel, dims), out_shape=(jax.Shape...]
    unnamed x4 -> x2, local copies, waits for them, and re-layouts: 4.14 us -> 0.01 us
    pallas_call x0 -> x1, Pallas kernels: none -> 2.31 us  [hand_over(): pl.pallas_call(functools.partial(hand_over_kernel, count), out_shape=tupl...]
where the time goes in v3:
time: 120 us
  Pallas kernels  112 us (93%)
  matrix products  5.05 us (4%)
  local copies, waits for them, and re-layouts  1.51 us (1%)
  between operations  1.45 us (1%)
    pallas_call x1, Pallas kernels, attend(): pl.pallas_call(functools.partial(main_kernel, dims), out_shape=(jax.Shape...  99.1 us
    pallas_call x1, Pallas kernels, pick(): pl.pallas_call(functools.partial(pick_kernel, wide, per_owner, capacity),...  10.6 us
    dot_general x2, matrix products, lookup(): jnp.dot(picked, table, preferred_element_type=jnp.float32)  5.05 us

profile of v3, /device:TPU:0, one launch (start us, length us, event | category | flops | bytes accessed | tf_op | source)
XLA Modules:
  0.0 120.0 jit_solution(6267219243604569485)
XLA Ops:
  0.6 0.0 copy-start
  1.4 0.9 broadcast_in_dim.7
  2.3 0.6 broadcast_in_dim.8.ids_ref
  2.9 10.6 %shard_map.104.picked_ref = bf16[256,500]{1,0:T(8,128)(2,1)} custom-call(s32[8,128]{1,0:T(8,128)} %broadcast_in_dim.8.ids_ref), custom_call_target="tpu_custom_call" | custom-call | tf_op jit(solution)/shard_map/pallas_call | solution.py:93
  13.6 1.9 %convolution_convert_fusion.1.kv_ref = bf16[256,256]{1,0:T(8,128)(2,1)} fusion(bf16[256,500]{1,0:T(8,128)(2,1)} %shard_map.104.picked_ref, bf16[500,256]{1,0:T(8,128)(2,1)} %param.16), kind=kOutput, calls=%fused_computation.1 | convolution fusion | flops 65601536 | bytes 643072 | tf_op jit(solution)/shard_map/dot_general | solution.py:612
  15.5 0.0 copy-done
  15.5 3.1 %convolution_convert_fusion.self_ref = bf16[256,3072]{1,0:T(8,128)(2,1)} fusion(bf16[256,500]{1,0:T(8,128)(2,1)} %shard_map.104.picked_ref, bf16[500,3072]{1,0:T(8,128)(2,1)S(1)} %copy-done), kind=kOutput, calls=%fused_computation | convolution fusion | flops 787218432 | bytes 4900864 | tf_op jit(solution)/shard_map/dot_general | solution.py:612
  18.6 99.1 %shard_map.105 = (bf16[128,3072]{1,0:T(8,128)(2,1)}, bf16[64,6144]{1,0:T(8,128)(2,1)}) custom-call(s32[1]{0:T(128)S(6)} %copy.11.problem_ref, s32[8,128]{1,0:T(8,128)} %broadcast_in_dim.8.ids_ref, bf16[192,3072]{1,0:T(8,128)(2,1)} %hidden_ref.1, f32[1,3072]{1,0:T(1,128)} %bitcast.9, bf16[3072,256]{1,0:T(8,128)(2,1)} %weight_ref.1, ...), custom_call_target="tpu_custom_call" | custom-call | tf_op jit(solution)/shard_map/pallas_call | solution.py:507
  117.7 2.3 %shard_map.106 = (bf16[128,3072]{1,0:T(8,128)(2,1)}, bf16[64,6144]{1,0:T(8,128)(2,1)}) custom-call(bf16[128,3072]{1,0:T(8,128)(2,1)} %get-tuple-element.6.refs_0_, bf16[64,6144]{1,0:T(8,128)(2,1)} %get-tuple-element.7.refs_1_), custom_call_target="tpu_custom_call" | custom-call | tf_op jit(solution)/shard_map/pallas_call | solution.py:580
Async XLA Ops:
  0.6 14.8 %copy-start = (bf16[500,3072]{1,0:T(8,128)(2,1)S(1)}, bf16[500,3072]{1,0:T(8,128)(2,1)}, u32[]{:S(2)}) copy-start(bf16[500,3072]{1,0:T(8,128)(2,1)} %param.15) | copy-start | bytes 9216004
